TPU v7x, 512 devices: a whole 4x8x8 slice. The times are simulated.
512 devices in a mesh: dp: 64 (over z, x, core), group: 8 (over y).
Axes of the slice: x: 4, y: 8, z: 8, core: 2. Of those that a mesh axis runs over, the one named last changes fastest.
Arguments:
- queries: bfloat16 [8192, 2, 2048], P('dp', None, 'group'), may hold values from -21 to 21
- new_keys: bfloat16 [8192, 2048], P('dp', 'group'), may hold values from -12 to 12
- new_values: bfloat16 [8192, 2048], P('dp', 'group'), may hold values from -6 to 6
- cache_keys: bfloat16 [64, 2048, 2048], P('dp', None, 'group'), may hold values from -6 to 6
- cache_values: bfloat16 [64, 2048, 2048], P('dp', None, 'group'), may hold values from -6 to 6
- lengths: int32 [64], P('dp'), may hold values from 1 to 2048, as said below
- att_gates: float32 [8192, 2], P('dp'), may hold values from 0.1 to 0.9
- resid: bfloat16 [8192, 2048], P('dp', 'group'), may hold values from -72 to 72
- norm_gain: float32 [2048], P('group'), may hold values from 0.5 to 1.5
- expert_ids: int32 [8192, 2], P('dp'), may hold values from 0 to 7, all different within a row; in each aligned block of 128 rows (0 to 127, 128 to 255, ...) at most 40 rows name the same one
- expert_gates: float32 [8192, 2], P('dp'), may hold values from 0.1 to 0.9
- w_gate: bfloat16 [64, 2048, 704], P('dp', 'group'), may hold values from -0.125 to 0.125
- w_up: bfloat16 [64, 2048, 704], P('dp', 'group'), may hold values from -0.125 to 0.125
- w_down: bfloat16 [64, 704, 2048], P('dp', None, 'group'), may hold values from -0.078125 to 0.078125
Outputs:
- attended: bfloat16 [8192, 2048], P('dp', 'group')
- mixed: bfloat16 [8192, 2048], P('dp', 'group')
Inputs may be any that keep to these rules, and one draw needn't show every extreme that they name: `expert_ids`: in the tokens of one request (aligned blocks of 128 rows) no expert is named more than 40 times, a bound that some block reaches; the two experts of a row differ. `lengths`: some request has exactly 2048 cached tokens.
All inputs are finite; a program needn't handle non-finite values.
Results may differ from a plain program's by a relative error of at most 0.0055.
Values may be sent and summed in bfloat16 or wider, within the bound.
No kernel may reach another device: no remote copies, remote signals or barrier semaphores. Data moves between devices by JAX's collectives and lax.ppermute only.
A program may use at most 64 MiB of HBM per device.

v0:
```python
import jax
import jax.numpy as jnp
from jax import lax
from jax.sharding import PartitionSpec as P

D = 2048
HD = 128
EXPERTS = 8
CACHE = 2048
CAP = 40


def pair_slots(expert_rows):
    flat_ids = expert_rows.reshape(-1)
    onehot = (flat_ids[:, None] == jnp.arange(EXPERTS, dtype=jnp.int32)[None, :]).astype(jnp.int32)
    running = jnp.cumsum(onehot, axis=0)
    return (jnp.sum(running * onehot, axis=1) - 1).reshape(expert_rows.shape)


def attend_local(queries, new_keys, new_values, cache_keys, cache_values, lengths, att_gates):
    row_count = queries.shape[0]
    local_heads = queries.shape[2] // HD
    query_h = queries.reshape(row_count, 2, local_heads, HD)
    key_new = new_keys.reshape(row_count, local_heads, HD)
    value_new = new_values.reshape(row_count, local_heads, HD)
    key_cache = cache_keys[0].reshape(CACHE, local_heads, HD)
    value_cache = cache_values[0].reshape(CACHE, local_heads, HD)
    length = lengths[0]
    score_scale = HD ** (-0.5)
    key_block = min(512, CACHE)
    blocks_live = (length + key_block - 1) // key_block

    def block_scores(block_index):
        keys_here = lax.dynamic_slice_in_dim(key_cache, block_index * key_block, key_block, 0)
        scores = (
            jnp.einsum("tshd,khd->shtk", query_h, keys_here, preferred_element_type=jnp.float32)
            * score_scale
        )
        position = block_index * key_block + jnp.arange(key_block, dtype=jnp.int32)
        return jnp.where(position[None, None, None, :] < length, scores, -jnp.inf)

    own_pos = jnp.arange(row_count, dtype=jnp.int32)
    causal = own_pos[None, :] <= own_pos[:, None]
    new_scores = (
        jnp.einsum("tshd,khd->shtk", query_h, key_new, preferred_element_type=jnp.float32)
        * score_scale
    )
    new_scores = jnp.where(causal[None, None], new_scores, -jnp.inf)
    row_max = jnp.max(new_scores, axis=-1)
    row_total = jnp.sum(jnp.exp(new_scores - row_max[..., None]), axis=-1)

    def stats_step(block_index, carry):
        old_max, old_total = carry
        scores = block_scores(block_index)
        new_max = jnp.maximum(old_max, jnp.max(scores, axis=-1))
        new_total = old_total * jnp.exp(old_max - new_max) + jnp.sum(
            jnp.exp(scores - new_max[..., None]), axis=-1
        )
        return (new_max, new_total)

    row_max, row_total = lax.fori_loop(0, blocks_live, stats_step, (row_max, row_total))

    def weigh(scores):
        return (jnp.exp(scores - row_max[..., None]) / row_total[..., None]).astype(jnp.bfloat16)

    output = jnp.einsum(
        "shtk,khd->tshd", weigh(new_scores), value_new, preferred_element_type=jnp.float32
    )

    def value_step(block_index, accum):
        values_here = lax.dynamic_slice_in_dim(value_cache, block_index * key_block, key_block, 0)
        return accum + jnp.einsum(
            "shtk,khd->tshd",
            weigh(block_scores(block_index)),
            values_here,
            preferred_element_type=jnp.float32,
        )

    output = lax.fori_loop(0, blocks_live, value_step, output)
    output = output.reshape(row_count, 2, local_heads * HD)
    return jnp.sum(output * att_gates[:, :, None], axis=1)


def on_device(
    queries,
    new_keys,
    new_values,
    cache_keys,
    cache_values,
    lengths,
    att_gates,
    resid,
    norm_gain,
    expert_ids,
    expert_gates,
    w_gate,
    w_up,
    w_down,
):
    row_count = queries.shape[0]
    attention = attend_local(
        queries, new_keys, new_values, cache_keys, cache_values, lengths, att_gates
    )
    attended = attention.astype(jnp.bfloat16)
    mixed_in = resid.astype(jnp.float32) + attention
    squares = lax.psum(jnp.sum(mixed_in * mixed_in, axis=1), "group")
    normed = (mixed_in / jnp.sqrt(squares[:, None] / D + 1e-05) * norm_gain[None, :]).astype(
        jnp.bfloat16
    )
    groups = lax.axis_size("group")
    owners = lax.axis_size("dp") // EXPERTS
    spread = owners * EXPERTS
    per_group = CAP // groups
    slot_index = pair_slots(expert_ids)
    slot_dest = expert_ids * CAP + slot_index
    slot_table = jnp.sum(
        (jnp.arange(EXPERTS * CAP, dtype=jnp.int32)[:, None, None] == slot_dest[None]).astype(
            jnp.bfloat16
        ),
        axis=2,
    )
    packed = jnp.dot(slot_table, normed, preferred_element_type=jnp.float32).astype(jnp.bfloat16)
    packed = packed.reshape(EXPERTS, 1, CAP, packed.shape[1])
    packed = jnp.broadcast_to(packed, (EXPERTS, owners, CAP, packed.shape[3])).reshape(
        spread, CAP, packed.shape[3]
    )
    arrived = lax.all_to_all(
        lax.all_to_all(packed, "dp", split_axis=0, concat_axis=0, tiled=True),
        "group",
        split_axis=1,
        concat_axis=2,
        tiled=True,
    )
    features = arrived.reshape(spread * per_group, arrived.shape[2])
    gate_act = jnp.dot(
        features,
        lax.all_gather(w_gate[0], "group", axis=0, tiled=True),
        preferred_element_type=jnp.float32,
    )
    up_act = jnp.dot(
        features,
        lax.all_gather(w_up[0], "group", axis=0, tiled=True),
        preferred_element_type=jnp.float32,
    )
    hidden = (jax.nn.silu(gate_act) * up_act).astype(jnp.bfloat16)
    partial_value = jnp.dot(
        hidden,
        lax.all_gather(w_down[0], "group", axis=1, tiled=True),
        preferred_element_type=jnp.float32,
    ).astype(jnp.bfloat16)
    partial_value = partial_value.reshape(spread, per_group, partial_value.shape[1])
    returned = lax.all_to_all(
        lax.all_to_all(partial_value, "dp", split_axis=0, concat_axis=0, tiled=True),
        "group",
        split_axis=2,
        concat_axis=1,
        tiled=True,
    )
    summed = jnp.sum(
        returned.reshape(EXPERTS, owners, CAP, returned.shape[2]).astype(jnp.float32), axis=1
    )
    summed = summed.reshape(EXPERTS * CAP, returned.shape[2])
    picked = jnp.take(summed, slot_dest.reshape(-1), axis=0).reshape(row_count, 2, summed.shape[1])
    expert_mix = jnp.sum(picked * expert_gates[:, :, None], axis=1)
    mixed = (mixed_in + expert_mix).astype(jnp.bfloat16)
    return (attended, mixed)


def solution(mesh):
    in_specs = (
        P("dp", None, "group"),
        P("dp", "group"),
        P("dp", "group"),
        P("dp", None, "group"),
        P("dp", None, "group"),
        P("dp"),
        P("dp", None),
        P("dp", "group"),
        P("group"),
        P("dp", None),
        P("dp", None),
        P("dp", "group", None),
        P("dp", "group", None),
        P("dp", None, "group"),
    )
    out_specs = (P("dp", "group"), P("dp", "group"))
    return jax.shard_map(
        on_device, mesh=mesh, in_specs=in_specs, out_specs=out_specs, check_vma=False
    )
```

profile of v0, /device:TPU:1, one launch (start us, length us, event | category | flops | bytes accessed | tf_op | source)
XLA Modules:
  0.0 349.8 jit_solution(9953822415055390720)
XLA Ops:
  9.3 1.0 copy.143
  10.5 0.9 reshape.139
  13.0 4.9 %while.22 = (s32[]{:T(128)}, f32[2,2,128]{2,0,1:T(2,128)S(1)}, f32[2,2,128]{2,0,1:T(2,128)S(1)}, s32[]{:T(128)}, s32[]{:T(128)}, /*index=5*/bf16[2048,2,128]{2,0...) while((s32[]{:T(128)}, f32[2,2,128]{2,0,1:T(2,128)S(1)}, ...), condition=%wide.region_5.6_spmd, body=%wide.region_2.5_spmd.sunk | while | flops 68421640 | bytes 2518183 | solution.py:61
  20.0 5.1 %while.23 = (s32[]{:T(128)}, f32[128,2,2,128]{0,3,1,2:T(8,128)S(1)}, s32[]{:T(128)}, bf16[2048,2,128]{0,2,1:T(8,128)(2,1)S(1)}, s32[]{:T(128)}, /*index=5*/bf16[...) while((s32[]{:T(128)}, ...), condition=%wide.region_7.8_spmd, body=%wide.region_6.7_spmd.sunk | while | flops 135595008 | bytes 1185971 | solution.py:79
  26.6 15.7 %psum.7 = f32[128]{0:T(128)S(1)} all-reduce(f32[128]{0:T(128)S(1)} %multiply_reduce_fusion.2), channel_id=1, replica_groups=mesh['dp'=64,'group'=8] {'group'}, use_global_device_ids=true, to_apply=%region_14.15 | all-reduce | flops 128 | bytes 1024 | tf_op jit(solution)/shard_map/psum | solution.py:106
  42.6 1.2 broadcast_in_dim.71
  43.8 16.8 %all-to-all-start = ((bf16[64,40,256]{2,1,0:T(8,128)(2,1)}), bf16[64,40,256]{2,1,0:T(8,128)(2,1)S(1)}, u32[]{:S(2)}, u32[]{:S(2)}) async-start(bf16[64,40,256]{2,1,0:T(8,128)(2,1)} %bitcast.21), calls=%async_computation | async-start | bytes 2621440 | tf_op jit(solution)/shard_map/all_to_all | solution.py:128
  61.4 32.9 %all-to-all-done = bf16[64,40,256]{2,1,0:T(8,128)(2,1)S(1)} async-done(((bf16[64,40,256]{2,1,0:T(8,128)(2,1)}), bf16[64,40,256]{2,1,0:T(8,128)(2,1)S(1)}, u32[]{:S(2)}, u32[]{:S(2)}) %all-to-all-start) | async-done | bytes 1310752 | tf_op jit(solution)/shard_map/all_to_all | solution.py:128
  94.5 46.3 %all_to_all.34 = bf16[64,40,256]{2,0,1:T(8,128)(2,1)S(1)} all-to-all(bf16[64,40,256]{2,0,1:T(8,128)(2,1)S(1)} %copy.161), channel_id=1, replica_groups=mesh['dp'=64,'group'=8] {'group'}, dimensions={1} | all-to-all | bytes 2621440 | tf_op jit(solution)/shard_map/all_to_all | solution.py:127
  142.0 4.1 %fusion.33 = f32[320,704]{1,0:T(8,128)} fusion(bf16[320,2048]{1,0:T(8,128)(2,1)S(1)} %bitcast.129, bf16[1,2048,704]{1,2,0:T(8,128)(2,1)} %all-gather.7.cloned.1.call-done), kind=kOutput, calls=%fused_computation.37 | convolution fusion | flops 922746880 | bytes 5095424 | tf_op jit(solution)/shard_map/dot_general | solution.py:135
  146.2 4.4 %all-gather.11.cloned.1.call-done = bf16[1,704,2048]{2,1,0:T(8,128)(2,1)} async-done(((bf16[1,704,256]{2,1,0:T(8,128)(2,1)}), bf16[1,704,2048]{2,1,0:T(8,128)(2,1)}) %all-gather.11.cloned.1.call-update) | async-done | bytes 2883600 | tf_op jit(solution)/shard_map/all_gather | solution.py:148
  150.6 56.6 %all-gather.9.cloned.1.call-done = bf16[1,2048,704]{1,2,0:T(8,128)(2,1)} async-done(((bf16[1,256,704]{1,2,0:T(8,128)(2,1)}), bf16[1,2048,704]{1,2,0:T(8,128)(2,1)}) %all-gather.9.cloned.1.call-update) | async-done | bytes 2883600 | tf_op jit(solution)/shard_map/all_gather | solution.py:142
  207.2 5.6 %fusion.35 = bf16[320,2048]{1,0:T(8,128)(2,1)S(1)} fusion(bf16[1,704,2048]{2,1,0:T(8,128)(2,1)} %all-gather.11.cloned.1.call-done, bf16[320,2048]{1,0:T(8,128)(2,1)S(1)} %bitcast.130, bf16[1,2048,704]{1,2,0:T(8,128)(2,1)} %all-gather.9.cloned.1.call-done, f32[320,704]{1,0:T(8,128)} %fusion.33), kind=kOutput, calls=%fused_computation.39 | convolution fusion | flops 1847500800 | bytes 9289728 | tf_op jit(solution)/shard_map/dot_general | solution.py:146
  212.9 1.6 reshape.145
  214.5 64.0 %all_to_all.35 = bf16[64,5,2048]{2,1,0:T(8,128)(2,1)S(1)} all-to-all(bf16[64,5,2048]{2,1,0:T(8,128)(2,1)} %reshape.145), channel_id=1, replica_groups=mesh['dp'=64,'group'=8] {'dp'}, dimensions={0} | all-to-all | bytes 2621440 | tf_op jit(solution)/shard_map/all_to_all | solution.py:153
  278.5 5.1 %copy.163 = bf16[64,5,2048]{0,1,2:T(8,128)(2,1)} copy(bf16[64,5,2048]{2,1,0:T(8,128)(2,1)S(1)} %all_to_all.35) | data formatting | bytes 2621440 | tf_op jit(solution)/shard_map/all_to_all | solution.py:153
  283.6 7.0 %reshape.167 = bf16[8,2,40960]{2,1,0:T(2,128)(2,1)} reshape(bf16[2048,5,64]{2,1,0:T(8,128)(2,1)} %bitcast.122) | data formatting | bytes 2621440
  290.6 4.5 %all-to-all-start.3 = ((bf16[8,2,40960]{2,1,0:T(2,128)(2,1)}), bf16[8,2,40960]{2,1,0:T(2,128)(2,1)S(1)}, u32[]{:S(2)}, u32[]{:S(2)}) async-start(bf16[8,2,40960]{2,1,0:T(2,128)(2,1)} %reshape.167), calls=%async_computation.3 | async-start | bytes 2621440 | tf_op jit(solution)/shard_map/all_to_all | solution.py:152
  295.6 34.3 %all-to-all-done.3 = bf16[8,2,40960]{2,1,0:T(2,128)(2,1)S(1)} async-done(((bf16[8,2,40960]{2,1,0:T(2,128)(2,1)}), bf16[8,2,40960]{2,1,0:T(2,128)(2,1)S(1)}, u32[]{:S(2)}, u32[]{:S(2)}) %all-to-all-start.3) | async-done | bytes 1310752 | tf_op jit(solution)/shard_map/all_to_all | solution.py:152
  329.9 4.8 %reshape.168 = bf16[2048,5,64]{2,1,0:T(8,128)(2,1)} reshape(bf16[8,2,40960]{2,1,0:T(2,128)(2,1)S(1)} %all-to-all-done.3) | data formatting | bytes 2621440
  334.7 4.0 %copy.164 = bf16[64,5,2048]{2,0,1:T(8,128)(2,1)S(1)} copy(bf16[64,5,2048]{0,1,2:T(8,128)(2,1)} %bitcast.123) | data formatting | bytes 2621440 | tf_op jit(solution)/shard_map/all_to_all | solution.py:152
  339.0 1.1 copy.184
  340.6 1.0 gather_fusion
  341.7 0.9 multiply_reduce_fusion
  (103 shorter events, 20.7 us)
Async XLA Ops:
  7.2 4.2 %copy-start = (bf16[1,2048,256]{2,1,0:T(8,128)(2,1)S(1)}, bf16[1,2048,256]{2,1,0:T(8,128)(2,1)}, u32[]{:S(2)}) copy-start(bf16[1,2048,256]{2,1,0:T(8,128)(2,1)} %param.21) | copy-start | bytes 3145732
  7.2 134.9 %all-gather.7.cloned.1.call-start = ((), (), s32[]{:S(2)}) async-start(), calls=%async_computation.4 | async-start | bytes 3244032 | tf_op jit(solution)/shard_map/all_gather | solution.py:137
  7.9 142.7 %all-gather.11.cloned.1.call-start = ((), (), s32[]{:S(2)}) async-start(), calls=%async_computation.6 | async-start | bytes 3244032 | tf_op jit(solution)/shard_map/all_gather | solution.py:148
  13.0 4.9 %copy-start.5 = (s32[128,2]{0,1:T(2,128)S(1)}, s32[128,2]{0,1:T(2,128)}, u32[]{:S(2)}) copy-start(s32[128,2]{0,1:T(2,128)} %param.27) | copy-start | bytes 3076
  13.0 5.9 %copy-start.4 = (bf16[128,256]{1,0:T(8,128)(2,1)S(1)}, bf16[128,256]{1,0:T(8,128)(2,1)}, u32[]{:S(2)}) copy-start(bf16[128,256]{1,0:T(8,128)(2,1)} %param.20) | copy-start | bytes 196612
  17.9 1.4 copy-start.1
  20.0 5.2 %copy-start.7 = (f32[128,2]{0,1:T(2,128)S(1)}, f32[128,2]{0,1:T(2,128)}, u32[]{:S(2)}) copy-start(f32[128,2]{0,1:T(2,128)} %param.24) | copy-start | bytes 3076
  20.0 6.2 %copy-start.6 = (s32[256]{0:T(256)S(1)}, s32[256]{0:T(256)}, u32[]{:S(2)}) copy-start(s32[256]{0:T(256)} %eq.38) | copy-start | bytes 3076
  20.0 6.5 %copy-start.2 = (bf16[128,256]{1,0:T(8,128)(2,1)S(1)}, bf16[128,256]{1,0:T(8,128)(2,1)}, u32[]{:S(2)}) copy-start(bf16[128,256]{1,0:T(8,128)(2,1)} %param.25) | copy-start | bytes 196612
  20.0 22.3 %copy-start.9 = (f32[256]{0:T(256)S(1)}, f32[256]{0:T(256)}, u32[]{:S(2)}) copy-start(f32[256]{0:T(256)} %param.26) | copy-start | bytes 3076
  43.8 50.4 %all-to-all-start = ((bf16[64,40,256]{2,1,0:T(8,128)(2,1)}), bf16[64,40,256]{2,1,0:T(8,128)(2,1)S(1)}, u32[]{:S(2)}, u32[]{:S(2)}) async-start(bf16[64,40,256]{2,1,0:T(8,128)(2,1)} %bitcast.21), calls=%async_computation | async-start | bytes 2621440 | tf_op jit(solution)/shard_map/all_to_all | solution.py:128
  60.6 146.6 %all-gather.9.cloned.1.call-start = ((), (), s32[]{:S(2)}) async-start(), calls=%async_computation.5 | async-start | bytes 3244032 | tf_op jit(solution)/shard_map/all_gather | solution.py:142
  290.6 4.9 %copy-start.8 = (f32[128,2]{0,1:T(2,128)S(1)}, f32[128,2]{0,1:T(2,128)}, u32[]{:S(2)}) copy-start(f32[128,2]{0,1:T(2,128)} %param.28) | copy-start | bytes 3076
  290.6 39.3 %all-to-all-start.3 = ((bf16[8,2,40960]{2,1,0:T(2,128)(2,1)}), bf16[8,2,40960]{2,1,0:T(2,128)(2,1)S(1)}, u32[]{:S(2)}, u32[]{:S(2)}) async-start(bf16[8,2,40960]{2,1,0:T(2,128)(2,1)} %reshape.167), calls=%async_computation.3 | async-start | bytes 2621440 | tf_op jit(solution)/shard_map/all_to_all | solution.py:152
  340.5 2.2 copy-start.3
Sparse Core Ops, SparseCore 0:
  10.0 58.7 all-gather.6
  70.8 79.7 all-gather.10
  152.6 54.5 all-gather.8
where the time goes:
time: 351 us; the launch traced here: 350 us
  waiting for transfers between devices  130 us (37%)
  blocking collectives  126 us (36%)
  local copies, waits for them, and re-layouts  33.8 us (10%)
  starting transfers between devices  21.4 us (6%)
  between operations  14.8 us (4%)
  matrix products  14.1 us (4%)
  other arithmetic  9.01 us (3%)
    all_to_all x1, blocking collectives, on_device(): lax.all_to_all(partial_value, 'dp', split_axis=0, concat_axis=0, tiled=True)  64 us
    all_gather x1, waiting for transfers between devices, on_device(): lax.all_gather(w_up[0], 'group', axis=0, tiled=True)  56.6 us
    all_to_all x1, blocking collectives, on_device(): lax.all_to_all(lax.all_to_all(packed, 'dp', split_axis=0, concat_axis=0,...  46.3 us
    all_to_all x1, waiting for transfers between devices, on_device(): lax.all_to_all(lax.all_to_all(partial_value, 'dp', split_axis=0, concat_a...  34.3 us
    all_to_all x1, waiting for transfers between devices, on_device(): lax.all_to_all(packed, 'dp', split_axis=0, concat_axis=0, tiled=True)  32.9 us
    all_to_all x1, starting transfers between devices, on_device(): lax.all_to_all(packed, 'dp', split_axis=0, concat_axis=0, tiled=True)  16.8 us
    unnamed x30, local copies, waits for them, and re-layouts  16.1 us
    psum x1, blocking collectives, on_device(): squares = lax.psum(jnp.sum(mixed_in * mixed_in, axis=1), 'group')  15.7 us
  transfers between devices with their start and end apart: 5, of which 4 were waited for; matrix products, arithmetic and copies ran while one was open for 7% of the time, Pallas kernels for 0%

commit v1 on v0

v1 whole, which is shorter than its diff:
```python
import jax
import jax.numpy as jnp
from jax import lax
from jax.experimental import pallas as pl
from jax.experimental.pallas import tpu as pltpu
from jax.sharding import Mesh, PartitionSpec as P

D = 2048
HD = 128
EXPERTS = 8
CACHE = 2048
CAP = 40
TOK = 128
FEAT = 256
FFB = 704
GROUPS = 8
PER = CAP // GROUPS
MAIN = 640
TAIL = FFB - MAIN
WIDE = 2 * FFB
SLOTS_W = PER * FEAT
SEND_W = SLOTS_W + 128
ROWS = 64
TROWS = PER * ROWS
VMEM = 56 * 1024 * 1024

f32 = jnp.float32
bf16 = jnp.bfloat16


def params():
    return pltpu.CompilerParams(vmem_limit_bytes=VMEM)


def pack_kernel(gate_ref, up_ref, down_ref, out_ref):
    out_ref[0:FEAT, 0:MAIN] = gate_ref[0, :, 0:MAIN]
    out_ref[0:FEAT, MAIN : 2 * MAIN] = up_ref[0, :, 0:MAIN]
    out_ref[0:FEAT, 2 * MAIN : WIDE] = jnp.concatenate(
        [gate_ref[0, :, MAIN:FFB], up_ref[0, :, MAIN:FFB]], axis=1
    )
    for q in range(MAIN // 128):
        out_ref[FEAT : FEAT + 128, q * 256 : (q + 1) * 256] = down_ref[0, q * 128 : (q + 1) * 128, :]
    out_ref[FEAT : FEAT + TAIL, 2 * MAIN : WIDE] = down_ref[0, MAIN:FFB, 0:128]
    out_ref[FEAT + TAIL : FEAT + 128, 2 * MAIN : WIDE] = down_ref[0, MAIN:FFB, 128:256]


def pack_weights(w_gate, w_up, w_down):
    return pl.pallas_call(
        pack_kernel,
        out_shape=jax.ShapeDtypeStruct((FEAT + 128, WIDE), bf16),
        compiler_params=params(),
        name="pack_weights",
    )(w_gate, w_up, w_down)


def slot_dests(ids):
    lane = lax.broadcasted_iota(jnp.int32, (TOK, 128), 1)
    row = lax.broadcasted_iota(jnp.int32, (TOK, 128), 0)
    first = ids[:, 0:1] == lane
    second = ids[:, 1:2] == lane
    named = jnp.where(first | second, 1.0, 0.0).astype(bf16)
    earlier = jnp.where(lane < row, 1.0, 0.0).astype(bf16)
    count = jnp.dot(earlier, named, preferred_element_type=f32)
    dest = []
    for k, hit in ((0, first), (1, second)):
        slot = jnp.sum(jnp.where(hit, count, 0.0), axis=1, keepdims=True).astype(jnp.int32)
        dest.append(ids[:, k : k + 1] * CAP + slot)
    return dest


def slot_values(i):
    lane = lax.broadcasted_iota(jnp.int32, (TOK, ROWS), 1)
    return (lane & 7) * CAP + (lane >> 3) * PER + i


def attend_kernel(
    len_ref, q_ref, kn_ref, vn_ref, kc_ref, vc_ref, ag_ref, res_ref, gain_ref, ids_ref,
    att_ref, mix_ref, send_ref,
):
    length = len_ref[0]
    neg = -1e30
    scale = HD ** (-0.5)
    live = lax.broadcasted_iota(jnp.int32, (TOK, CACHE), 1) < length
    causal = lax.broadcasted_iota(jnp.int32, (TOK, TOK), 1) <= lax.broadcasted_iota(jnp.int32, (TOK, TOK), 0)
    gates = ag_ref[...]
    nt = (((1,), (1,)), ((), ()))
    heads = []
    for h in range(FEAT // HD):
        cols = slice(h * HD, (h + 1) * HD)
        key_c, val_c = kc_ref[0, :, cols], vc_ref[0, :, cols]
        key_n, val_n = kn_ref[:, cols], vn_ref[:, cols]
        mixed_head = jnp.zeros((TOK, HD), f32)
        for s in range(2):
            q = q_ref[:, s * FEAT + h * HD : s * FEAT + (h + 1) * HD]
            sc = lax.dot_general(q, key_c, nt, preferred_element_type=f32) * scale
            sc = jnp.where(live, sc, neg)
            sn = lax.dot_general(q, key_n, nt, preferred_element_type=f32) * scale
            sn = jnp.where(causal, sn, neg)
            top = jnp.maximum(jnp.max(sc, axis=1, keepdims=True), jnp.max(sn, axis=1, keepdims=True))
            pc = jnp.exp(sc - top)
            pn = jnp.exp(sn - top)
            inv = 1.0 / (jnp.sum(pc, axis=1, keepdims=True) + jnp.sum(pn, axis=1, keepdims=True))
            out = jnp.dot((pc * inv).astype(bf16), val_c, preferred_element_type=f32)
            out = out + jnp.dot((pn * inv).astype(bf16), val_n, preferred_element_type=f32)
            mixed_head = mixed_head + gates[:, s : s + 1] * out
        heads.append(mixed_head)
    attention = jnp.concatenate(heads, axis=1)
    att_ref[...] = attention.astype(bf16)
    mixed_in = res_ref[...].astype(f32) + attention
    mix_ref[...] = mixed_in
    scaled = (mixed_in * gain_ref[...]).astype(bf16)
    square = jnp.sum(mixed_in * mixed_in, axis=1, keepdims=True)
    high = square.astype(bf16).astype(f32)
    mid = (square - high).astype(bf16).astype(f32)
    low = square - high - mid
    dest = slot_dests(ids_ref[...])
    tn = (((0,), (0,)), ((), ()))
    lane = lax.broadcasted_iota(jnp.int32, (TOK, 128), 1)
    squares = jnp.zeros((ROWS, 128), f32)
    for i in range(PER):
        value = slot_values(i)
        pick = jnp.where((dest[0] == value) | (dest[1] == value), 1.0, 0.0).astype(bf16)
        block = lax.dot_general(pick, scaled, tn, preferred_element_type=f32)
        send_ref[:, i * FEAT : (i + 1) * FEAT] = block.astype(bf16)
        parts = jnp.where(lane == 3 * i, high, jnp.where(lane == 3 * i + 1, mid, jnp.where(lane == 3 * i + 2, low, 0.0)))
        squares = squares + lax.dot_general(pick, parts.astype(bf16), tn, preferred_element_type=f32)
    send_ref[:, SLOTS_W:SEND_W] = squares.astype(bf16)


def attend(length, q, kn, vn, kc, vc, ag, res, gain, ids):
    vm = pl.BlockSpec(memory_space=pltpu.VMEM)
    return pl.pallas_call(
        attend_kernel,
        in_specs=[pl.BlockSpec(memory_space=pltpu.SMEM)] + [vm] * 9,
        out_specs=[vm] * 3,
        out_shape=[
            jax.ShapeDtypeStruct((TOK, FEAT), bf16),
            jax.ShapeDtypeStruct((TOK, FEAT), f32),
            jax.ShapeDtypeStruct((ROWS, SEND_W), bf16),
        ],
        compiler_params=params(),
        name="attend",
    )(length, q, kn, vn, kc, vc, ag, res, gain, ids)


def arrange_kernel(got_ref, x_ref, inv_ref):
    total = jnp.zeros((8, 8, 128), f32)
    for f in range(8):
        rows = slice(f * 8, (f + 1) * 8)
        for i in range(PER):
            piece = got_ref[:, rows, i * FEAT : (i + 1) * FEAT].astype(f32).reshape(ROWS, FEAT)
            x_ref[f, i * ROWS : (i + 1) * ROWS, :] = piece.astype(bf16)
        total = total + got_ref[:, rows, SLOTS_W:SEND_W].astype(f32)
    total = total.reshape(ROWS, 128)
    lane = lax.broadcasted_iota(jnp.int32, (ROWS, 128), 1)
    for i in range(PER):
        mine = (lane >= 3 * i) & (lane < 3 * i + 3)
        square = jnp.sum(jnp.where(mine, total, 0.0), axis=1, keepdims=True)
        inv_ref[i * ROWS : (i + 1) * ROWS, :] = jnp.broadcast_to(1.0 / jnp.sqrt(square / D + 1e-05), (ROWS, 128))


def arrange(got):
    return pl.pallas_call(
        arrange_kernel,
        out_shape=[
            jax.ShapeDtypeStruct((8, TROWS, FEAT), bf16),
            jax.ShapeDtypeStruct((TROWS, 128), f32),
        ],
        compiler_params=params(),
        name="arrange",
    )(got)


def expert_kernel(x_ref, inv_ref, w_ref, out_ref, w_vm, act_vm, sems):
    copies = []
    for f in range(8):
        copies.append(pltpu.make_async_copy(w_ref.at[f, 0:FEAT], w_vm.at[f, 0:FEAT], sems.at[f]))
    for f in range(8):
        copies.append(
            pltpu.make_async_copy(w_ref.at[f, FEAT : FEAT + 128], w_vm.at[f, FEAT : FEAT + 128], sems.at[8 + f])
        )
    for copy in copies:
        copy.start()
    for f in range(8):
        copies[f].wait()
        part = jnp.dot(x_ref[f], w_vm[f, 0:FEAT, :], preferred_element_type=f32)
        if f == 0:
            act_vm[...] = part
        else:
            act_vm[...] += part
    inv = inv_ref[:, 0:1]
    gate = act_vm[:, 0:MAIN] * inv
    up = act_vm[:, MAIN : 2 * MAIN] * inv
    main = (gate * jax.nn.sigmoid(gate) * up).astype(bf16)
    rest = act_vm[:, 2 * MAIN : WIDE] * inv
    gate_t, up_t = rest[:, 0:TAIL], rest[:, TAIL : 2 * TAIL]
    tail = (gate_t * jax.nn.sigmoid(gate_t) * up_t).astype(bf16)
    for f in range(8):
        copies[8 + f].wait()
        wd = jnp.concatenate([w_vm[f, FEAT : FEAT + 128, q * 256 : (q + 1) * 256] for q in range(MAIN // 128)], axis=0)
        wt = jnp.concatenate(
            [w_vm[f, FEAT : FEAT + TAIL, 2 * MAIN : WIDE], w_vm[f, FEAT + TAIL : FEAT + 128, 2 * MAIN : WIDE]], axis=1
        )
        res = jnp.dot(main, wd, preferred_element_type=f32) + jnp.dot(tail, wt, preferred_element_type=f32)
        for i in range(PER):
            piece = res[i * ROWS : (i + 1) * ROWS, :].reshape(8, 8, FEAT)
            out_ref[:, f * 8 : (f + 1) * 8, i * FEAT : (i + 1) * FEAT] = piece.astype(bf16)


def experts(x, inv, weights):
    vm = pl.BlockSpec(memory_space=pltpu.VMEM)
    return pl.pallas_call(
        expert_kernel,
        in_specs=[vm, vm, pl.BlockSpec(memory_space=pl.ANY)],
        out_specs=vm,
        out_shape=jax.ShapeDtypeStruct((8, ROWS, SLOTS_W), bf16),
        scratch_shapes=[
            pltpu.VMEM((8, FEAT + 128, WIDE), bf16),
            pltpu.VMEM((TROWS, WIDE), f32),
            pltpu.SemaphoreType.DMA((16,)),
        ],
        compiler_params=params(),
        name="experts",
    )(x, inv, weights)


def reduce_kernel(got_ref, out_ref):
    total = got_ref[0].astype(f32)
    for j in range(1, 8):
        total = total + got_ref[j].astype(f32)
    out_ref[...] = total.astype(bf16)


def reduce_parts(got):
    return pl.pallas_call(
        reduce_kernel,
        out_shape=jax.ShapeDtypeStruct((ROWS, SLOTS_W), bf16),
        compiler_params=params(),
        name="reduce_parts",
    )(got)


def combine_kernel(got_ref, mix_ref, ids_ref, eg_ref, out_ref):
    dest = slot_dests(ids_ref[...])
    gates = eg_ref[...]
    total = mix_ref[...]
    for k in range(2):
        picked = jnp.zeros((TOK, FEAT), f32)
        for i in range(PER):
            pick = jnp.where(dest[k] == slot_values(i), 1.0, 0.0).astype(bf16)
            picked = picked + jnp.dot(pick, got_ref[:, i * FEAT : (i + 1) * FEAT], preferred_element_type=f32)
        total = total + gates[:, k : k + 1] * picked
    out_ref[...] = total.astype(bf16)


def combine(got, mixed_in, ids, gates):
    return pl.pallas_call(
        combine_kernel,
        out_shape=jax.ShapeDtypeStruct((TOK, FEAT), bf16),
        compiler_params=params(),
        name="combine",
    )(got, mixed_in, ids, gates)


def on_device(
    queries, new_keys, new_values, cache_keys, cache_values, lengths, att_gates, resid, norm_gain,
    expert_ids, expert_gates, w_gate, w_up, w_down,
):
    packed = pack_weights(w_gate, w_up, w_down)
    weights = lax.all_gather(packed, "y")
    attended, mixed_in, send = attend(
        lengths, queries.reshape(TOK, 2 * FEAT), new_keys, new_values, cache_keys, cache_values,
        att_gates, resid, norm_gain.reshape(1, FEAT), expert_ids,
    )
    got = lax.all_to_all(send, ("y", "z"), 0, 0, tiled=True)
    got = jnp.broadcast_to(got[None], (8, ROWS, SEND_W))
    got = lax.all_to_all(got, ("x", "c"), 0, 0, tiled=True)
    x, inv = arrange(got)
    part = experts(x, inv, weights)
    part = lax.all_to_all(part, ("x", "c"), 0, 0, tiled=True)
    done = reduce_parts(part)
    done = lax.all_to_all(done, ("y", "z"), 0, 0, tiled=True)
    mixed = combine(done, mixed_in, expert_ids, expert_gates)
    return attended, mixed


def solution(mesh):
    grid = Mesh(mesh.devices.reshape(8, 4, 2, 8), ("z", "x", "c", "y"))
    dp = ("z", "x", "c")
    in_specs = (
        P(dp, None, "y"),
        P(dp, "y"),
        P(dp, "y"),
        P(dp, None, "y"),
        P(dp, None, "y"),
        P(dp),
        P(dp, None),
        P(dp, "y"),
        P("y"),
        P(dp, None),
        P(dp, None),
        P(dp, "y", None),
        P(dp, "y", None),
        P(dp, None, "y"),
    )
    out_specs = (P(dp, "y"), P(dp, "y"))
    return jax.shard_map(on_device, mesh=grid, in_specs=in_specs, out_specs=out_specs, check_vma=False)
```

time: 351 us -> 193 us (0.55)
  waiting for transfers between devices: 130 us -> 48 us
  blocking collectives: 126 us -> 80.6 us
  Pallas kernels: 0 us -> 25.6 us
  local copies, waits for them, and re-layouts: 33.8 us -> 9.3 us
  matrix products: 14.1 us -> 0 us
  starting transfers between devices: 21.4 us -> 10.8 us
  other arithmetic: 9.01 us -> 3.22 us
    all_to_all x2 -> x1, waiting for transfers between devices: 67.1 us -> 11 us  [on_device(): done = lax.all_to_all(done, ('y', 'z'), 0, 0, tiled=True)]
    all_to_all x2 -> x3, blocking collectives: 110 us -> 80.6 us  [the longest x1 31.1 us: on_device(): got = lax.all_to_all(send, ('y', 'z'), 0, 0, tiled=True)]
    pallas_call x0 -> x6, Pallas kernels: none -> 25.6 us  [the longest x1 10 us: experts(): pl.pallas_call(expert_kernel, in_specs=[vm, vm, pl.BlockSpec(memory_space...]
    all_gather x3 -> x1, waiting for transfers between devices: 61.1 us -> 37 us  [on_device(): weights = lax.all_gather(packed, 'y')]
    psum x1 -> x0, blocking collectives: 15.7 us -> none  [on_device(): squares = lax.psum(jnp.sum(mixed_in * mixed_in, axis=1), 'group')]
    dot_general x13 -> x0, matrix products: 14.1 us -> none  [the longest x1 5.61 us: on_device(): jnp.dot(hidden, lax.all_gather(w_down[0], 'group', axis=1, tiled=True), p...]
    all_to_all x2 -> x1, starting transfers between devices: 21.3 us -> 10.7 us  [on_device(): done = lax.all_to_all(done, ('y', 'z'), 0, 0, tiled=True)]
    all_to_all x4 -> x1, local copies, waits for them, and re-layouts: 10.1 us -> 0.51 us  [on_device(): got = lax.all_to_all(send, ('y', 'z'), 0, 0, tiled=True)]
  transfers between devices with their start and end apart: 5 -> 2, of which waited for: 4 -> 2; matrix products, arithmetic and copies ran while one was open for 7% -> 3% of each run, Pallas kernels for 0% -> 4%
where the time goes in v1:
time: 193 us; the launch traced here: 192 us
  blocking collectives  80.6 us (42%)
  waiting for transfers between devices  48 us (25%)
  Pallas kernels  25.6 us (13%)
  between operations  14.8 us (8%)
  starting transfers between devices  10.8 us (6%)
  local copies, waits for them, and re-layouts  9.3 us (5%)
  other arithmetic  3.22 us (2%)
    all_gather x1, waiting for transfers between devices, on_device(): weights = lax.all_gather(packed, 'y')  37 us
    all_to_all x1, blocking collectives, on_device(): got = lax.all_to_all(send, ('y', 'z'), 0, 0, tiled=True)  31.1 us
    all_to_all x1, blocking collectives, on_device(): got = lax.all_to_all(got, ('x', 'c'), 0, 0, tiled=True)  26.5 us
    all_to_all x1, blocking collectives, on_device(): part = lax.all_to_all(part, ('x', 'c'), 0, 0, tiled=True)  23 us
    all_to_all x1, waiting for transfers between devices, on_device(): done = lax.all_to_all(done, ('y', 'z'), 0, 0, tiled=True)  11 us
    all_to_all x1, starting transfers between devices, on_device(): done = lax.all_to_all(done, ('y', 'z'), 0, 0, tiled=True)  10.7 us
    pallas_call x1, Pallas kernels, experts(): pl.pallas_call(expert_kernel, in_specs=[vm, vm, pl.BlockSpec(memory_space...  10 us
    unnamed x20, local copies, waits for them, and re-layouts  8.67 us
  transfers between devices with their start and end apart: 2, of which 2 were waited for; matrix products, arithmetic and copies ran while one was open for 3% of the time, Pallas kernels for 4%

profile of v1, /device:TPU:1, one launch (start us, length us, event | category | flops | bytes accessed | tf_op | source)
XLA Modules:
  0.0 192.2 jit_solution(13649774340134039638)
XLA Ops:
  7.2 1.9 copy.33.gate_ref
  9.1 1.9 copy.34.up_ref
  11.0 2.3 %pack_weights.1 = bf16[384,1408]{1,0:T(8,128)(2,1)} custom-call(bf16[1,256,704]{2,1,0:T(8,128)(2,1)} %copy.33.gate_ref, bf16[1,256,704]{2,1,0:T(8,128)(2,1)} %copy.34.up_ref, bf16[1,704,256]{2,1,0:T(8,128)(2,1)} %down_ref.1), custom_call_target="tpu_custom_call" | custom-call | tf_op jit(solution)/shard_map/pack_weights/pallas_call | solution.py:48
  13.4 0.7 copy.31.ids_ref
  14.1 0.7 copy.40
  14.8 0.7 copy.30.ag_ref
  16.2 6.0 %attend.1 = (bf16[128,256]{1,0:T(8,128)(2,1)}, f32[128,256]{1,0:T(8,128)}, bf16[64,1408]{1,0:T(8,128)(2,1)}) custom-call(s32[1]{0:T(128)S(6)} %copy.47.len_ref, bf16[128,512]{1,0:T(8,128)(2,1)} %bitcast.16, bf16[128,256]{1,0:T(8,128)(2,1)} %kn_ref.1, bf16[128,256]{1,0:T(8,128)(2,1)} %vn_ref.1, bf16[1,2048,256]{2,1,0:T(8,128)(2,1)} %kc_ref.1, ...), custom_call_target="tpu_custom_call" | custom-call | tf_op jit(solution)/shard_map/attend/pallas_call | solution.py:132
  22.1 0.5 broadcast
  22.7 1.6 reduce
  24.5 31.1 %all_to_all.30 = bf16[64,2,704]{2,1,0:T(2,128)(2,1)S(1)} all-to-all(bf16[64,2,704]{2,1,0:T(2,128)(2,1)S(1)} %reshape.19), channel_id=1, replica_groups=mesh['z'=8,'x'=4,'c'=2,'y'=8] {'y','z'}, dimensions={0} | all-to-all | bytes 360448 | tf_op jit(solution)/shard_map/all_to_all | solution.py:275
  55.6 0.2 reshape.20
  56.0 26.5 %all_to_all.31.got_ref = bf16[8,64,1408]{2,1,0:T(8,128)(2,1)} all-to-all(bf16[8,64,1408]{2,1,0:T(8,128)(2,1)S(1)} %broadcast_in_dim.9), channel_id=1, replica_groups=mesh['z'=8,'x'=4,'c'=2,'y'=8] {'x','c'}, dimensions={0} | all-to-all | bytes 2883584 | tf_op jit(solution)/shard_map/all_to_all | solution.py:277
  82.5 2.7 %arrange.1 = (bf16[8,320,256]{2,1,0:T(8,128)(2,1)}, f32[320,128]{1,0:T(8,128)}) custom-call(bf16[8,64,1408]{2,1,0:T(8,128)(2,1)} %all_to_all.31.got_ref), custom_call_target="tpu_custom_call" | custom-call | tf_op jit(solution)/shard_map/arrange/pallas_call | solution.py:163
  85.2 37.0 %all-gather.3.cloned.1.call-done = bf16[3072,1408]{1,0:T(8,128)(2,1)} async-done(((bf16[384,1408]{1,0:T(8,128)(2,1)}), bf16[3072,1408]{1,0:T(8,128)(2,1)}) %all-gather.3.cloned.1.call-update) | async-done | bytes 8650768 | tf_op jit(solution)/shard_map/all_gather | solution.py:270
  122.1 10.0 %experts.1 = bf16[8,64,1280]{2,1,0:T(8,128)(2,1)} custom-call(bf16[8,320,256]{2,1,0:T(8,128)(2,1)} %get-tuple-element.9.x_ref, f32[320,128]{1,0:T(8,128)} %get-tuple-element.10.inv_ref, bf16[8,384,1408]{2,1,0:T(8,128)(2,1)} %bitcast.12), custom_call_target="tpu_custom_call" | custom-call | tf_op jit(solution)/shard_map/experts/pallas_call | solution.py:212
  132.2 23.0 %all_to_all.32.got_ref = bf16[8,64,1280]{2,1,0:T(8,128)(2,1)} all-to-all(bf16[8,64,1280]{2,1,0:T(8,128)(2,1)} %experts.1), channel_id=1, replica_groups=mesh['z'=8,'x'=4,'c'=2,'y'=8] {'x','c'}, dimensions={0} | all-to-all | bytes 2621440 | tf_op jit(solution)/shard_map/all_to_all | solution.py:280
  155.2 2.2 %reduce_parts.1 = bf16[64,1280]{1,0:T(8,128)(2,1)} custom-call(bf16[8,64,1280]{2,1,0:T(8,128)(2,1)} %all_to_all.32.got_ref), custom_call_target="tpu_custom_call" | custom-call | tf_op jit(solution)/shard_map/reduce_parts/pallas_call | solution.py:235
  157.3 1.6 reduce.1
  158.9 0.7 reshape.21
  159.6 10.7 %all-to-all-start.3 = ((bf16[64,2,640]{2,1,0:T(2,128)(2,1)}), bf16[64,2,640]{2,1,0:T(2,128)(2,1)S(1)}, u32[]{:S(2)}, u32[]{:S(2)}) async-start(bf16[64,2,640]{2,1,0:T(2,128)(2,1)} %reshape.21), calls=%async_computation.3 | async-start | bytes 327680 | tf_op jit(solution)/shard_map/all_to_all | solution.py:282
  170.4 0.7 copy.37.eg_ref
  171.1 11.0 %all-to-all-done.3 = bf16[64,2,640]{2,1,0:T(2,128)(2,1)S(1)} async-done(((bf16[64,2,640]{2,1,0:T(2,128)(2,1)}), bf16[64,2,640]{2,1,0:T(2,128)(2,1)S(1)}, u32[]{:S(2)}, u32[]{:S(2)}) %all-to-all-start.3) | async-done | bytes 163872 | tf_op jit(solution)/shard_map/all_to_all | solution.py:282
  182.3 0.7 copy.44
  183.0 2.4 %combine.1 = bf16[128,256]{1,0:T(8,128)(2,1)} custom-call(bf16[64,1280]{1,0:T(8,128)(2,1)} %bitcast.14, f32[128,256]{1,0:T(8,128)} %get-tuple-element.11.mix_ref, s32[128,2]{1,0:T(8,128)} %copy.31.ids_ref, f32[128,2]{1,0:T(8,128)} %copy.37.eg_ref), custom_call_target="tpu_custom_call" | custom-call | tf_op jit(solution)/shard_map/combine/pallas_call | solution.py:257
  (14 shorter events, 0.5 us)
Async XLA Ops:
  7.2 115.0 %all-gather.3.cloned.1.call-start = ((), (), s32[]{:S(2)}) async-start(), calls=%async_computation.4 | async-start | bytes 9732096 | tf_op jit(solution)/shard_map/all_gather | solution.py:270
  11.0 2.4 %copy-start.1 = (s32[128,2]{0,1:T(2,128)S(1)}, s32[128,2]{0,1:T(2,128)}, u32[]{:S(2)}) copy-start(s32[128,2]{0,1:T(2,128)} %param.23) | copy-start | bytes 3076
  11.0 3.1 %copy-start = (bf16[128,2,256]{2,1,0:T(2,128)(2,1)S(1)}, bf16[128,2,256]{2,1,0:T(2,128)(2,1)}, u32[]{:S(2)}) copy-start(bf16[128,2,256]{2,1,0:T(2,128)(2,1)} %param.14) | copy-start | bytes 393220
  11.0 3.8 %copy-start.2 = (f32[128,2]{0,1:T(2,128)S(1)}, f32[128,2]{0,1:T(2,128)}, u32[]{:S(2)}) copy-start(f32[128,2]{0,1:T(2,128)} %param.20) | copy-start | bytes 3076
  155.2 15.2 %copy-start.3 = (f32[128,2]{0,1:T(2,128)S(1)}, f32[128,2]{0,1:T(2,128)}, u32[]{:S(2)}) copy-start(f32[128,2]{0,1:T(2,128)} %param.24) | copy-start | bytes 3076
  159.6 22.5 %all-to-all-start.3 = ((bf16[64,2,640]{2,1,0:T(2,128)(2,1)}), bf16[64,2,640]{2,1,0:T(2,128)(2,1)S(1)}, u32[]{:S(2)}, u32[]{:S(2)}) async-start(bf16[64,2,640]{2,1,0:T(2,128)(2,1)} %reshape.21), calls=%async_computation.3 | async-start | bytes 327680 | tf_op jit(solution)/shard_map/all_to_all | solution.py:282
Sparse Core Ops, SparseCore 0:
  13.5 108.6 all-gather.2
